TPU v7x, 128 devices: a whole 4x4x4 slice. The times are simulated.
128 devices in a mesh: seg: 64 (over y, z, x_hi, core), blk: 2 (over x_lo).
Axes of the slice: x: 4 (x_hi: 2, x_lo: 2; x = x_hi * 2 + x_lo), y: 4, z: 4, core: 2. Of those that a mesh axis runs over, the one named last changes fastest.
Arguments:
- state: bfloat16 [64, 4, 128, 2048], P('seg', 'blk'), may hold values from -6 to 6
- left_env: bfloat16 [64, 14, 4, 128, 128], P('seg', None, 'blk'), may hold values from -5 to 5
- right_env: bfloat16 [64, 14, 4, 128, 128], P('seg', None, 'blk'), may hold values from -3 to 3
- site_ops: bfloat16 [64, 14, 16, 16], P('seg'), may hold values from -4 to 4
- sector_map: int32 [64, 14, 4], P('seg'), may hold values from 0 to 3, as said below
- ranks: int32 [64, 4], P('seg', 'blk'), may hold values from 1 to 128
Outputs:
- new_state: bfloat16 [64, 4, 128, 2048], P('seg', 'blk')
- from_left: float32 [64, 14, 4, 128, 128], P('seg', None, 'blk')
- from_right: float32 [64, 14, 4, 128, 128], P('seg', None, 'blk')
Inputs may be any that keep to these rules, and one draw needn't show every extreme that they name: `sector_map`: channel 0 carries every block into itself; the other channels' source blocks are arbitrary.
All inputs are finite; a program needn't handle non-finite values.
Results may differ from a plain program's by a relative error of at most 0.012.
Values may be sent and summed in bfloat16 or wider, within the bound.
A program may use at most 192 MiB of HBM per device.

v0:
```python
import functools
import math

import jax
import jax.numpy as jnp
from jax import lax
from jax.experimental import pallas as pl
from jax.experimental.pallas import tpu as pltpu
from jax.sharding import PartitionSpec as P

STEP_SIZE = 0.25
EPSILON = 1e-06
MESH = pl.DeviceIdType.MESH
BF16 = jnp.bfloat16
F32 = jnp.float32


def dot(a, b):
    return jnp.dot(a, b, preferred_element_type=F32)


def kernel(dims, *refs):
    segs, chan, phys, blk, rows, chunks = dims
    wide = phys * blk
    tall = phys * rows
    pairs = chan // 2
    (state_ref, left_ref, right_ref, ops_ref, map_ref, ranks_ref, new_ref, recv_ref) = refs[:8]
    x = refs[8 : 8 + chunks]
    (env, lcat, kron, rdiag, z, img, wave, mixbuf, outbuf, sums, got) = refs[8 + chunks : 19 + chunks]
    (in_sem, own_sem, xs_sem, xr_sem, es_sem, er_sem, ss_sem, sr_sem) = refs[19 + chunks :]

    seg = lax.axis_index("seg")
    group = lax.axis_index("blk")
    other = 1 - group
    following = lax.rem(seg + 1, segs)
    previous = lax.rem(seg + segs - 1, segs)
    partner = (seg, other)

    own_copies = [
        pltpu.make_async_copy(
            state_ref.at[0, :, pl.ds(g * rows, rows), :], x[g].at[pl.ds(0, 2)], own_sem.at[g]
        )
        for g in range(chunks)
    ]
    left_copy = pltpu.make_async_copy(left_ref.at[0], env.at[0], in_sem.at[0])
    right_copy = pltpu.make_async_copy(right_ref.at[0], env.at[1], in_sem.at[1])
    barrier = pltpu.get_barrier_semaphore()
    for where in ((seg, other), (following, group), (previous, group)):
        pl.semaphore_signal(barrier, inc=1, device_id=where, device_id_type=MESH)
    right_copy.start()
    left_copy.start()
    for copy in own_copies:
        copy.start()
    pl.semaphore_wait(barrier, 3)

    def exchange(g, source):
        return pltpu.make_async_remote_copy(
            src_ref=source,
            dst_ref=x[g].at[pl.ds(2, 2)],
            send_sem=xs_sem.at[g],
            recv_sem=xr_sem.at[g],
            device_id=partner,
            device_id_type=MESH,
        )

    sends = [exchange(g, state_ref.at[0, :, pl.ds(g * rows, rows), :]) for g in range(chunks)]
    for copy in sends:
        copy.start()

    line = lax.broadcasted_iota(jnp.int32, (tall, phys), 0)
    pick = lax.broadcasted_iota(jnp.int32, (tall, phys), 1)
    spread_rows = (line // rows == pick).astype(BF16)
    line = lax.broadcasted_iota(jnp.int32, (phys, tall), 1)
    pick = lax.broadcasted_iota(jnp.int32, (phys, tall), 0)
    spread_cols = (line // rows == pick).astype(BF16)
    same = lax.broadcasted_iota(jnp.int32, (tall, tall), 0) % rows == (
        lax.broadcasted_iota(jnp.int32, (tall, tall), 1) % rows
    )

    def build_kron(k, carry):
        tall_op = dot(spread_rows, ops_ref[0, k]).astype(BF16)
        full = dot(tall_op, spread_cols)
        kron[k] = jnp.where(same, full, 0.0).astype(BF16)
        return carry

    lax.fori_loop(0, chan, build_kron, 0)

    right_copy.wait()

    def build_rdiag(k, carry):
        zeros = jnp.zeros((blk, blk), BF16)
        for b in range(2):
            turned = env[1, k, b].astype(F32).T.astype(BF16)
            rdiag[k, b * blk : (b + 1) * blk, b * blk : (b + 1) * blk] = turned
            rdiag[k, b * blk : (b + 1) * blk, (1 - b) * blk : (2 - b) * blk] = zeros
        return carry

    lax.fori_loop(0, chan, build_rdiag, 0)

    left_copy.wait()
    for k in range(chan):
        for b in range(2):
            lcat[b, :, k * blk : (k + 1) * blk] = env[0, k, b]

    def tiles(slab):
        return [slab[:, p * blk : (p + 1) * blk] for p in range(phys)]

    def contract(g):
        def one(k, carry):
            spots = [
                lax.rem(map_ref[0, k, 2 * group + b] + 4 - 2 * group, 4) for b in range(2)
            ]
            source = jnp.concatenate(
                [jnp.concatenate(tiles(x[g][spot]), axis=0) for spot in spots], axis=1
            )
            mixed = dot(kron[k], source).astype(BF16)
            part = dot(mixed, rdiag[k]).astype(BF16)
            row = pl.multiple_of(k * blk + g * rows, rows)
            for b in range(2):
                for p in range(phys):
                    z[b, pl.ds(row, rows), p * blk : (p + 1) * blk] = part[
                        p * rows : (p + 1) * rows, b * blk : (b + 1) * blk
                    ]
            return carry

        lax.fori_loop(0, chan, one, 0, unroll=2)

    def finish_image():
        for b in range(2):

            def one(n, carry):
                cols = pl.ds(pl.multiple_of(n * 256, 256), 256)
                img[b, :, cols] = dot(lcat[b], z[b, :, cols])
                return carry

            lax.fori_loop(0, wide // 256, one, 0)

    def fold(product):
        both = product[0] + product[1]
        total = both[:, :blk]
        for p in range(1, phys):
            total = total + both[:, p * blk : (p + 1) * blk]
        return total

    def rows_of(g):
        return slice(g * rows, (g + 1) * rows)

    def pair_total(slot, parts):
        for i, part in enumerate(parts):
            sums[slot, i] = part
        count = len(parts)
        copy = pltpu.make_async_remote_copy(
            src_ref=sums.at[slot, pl.ds(0, count)],
            dst_ref=got.at[slot, pl.ds(0, count)],
            send_sem=ss_sem.at[slot],
            recv_sem=sr_sem.at[slot],
            device_id=partner,
            device_id_type=MESH,
        )
        copy.start()
        copy.wait()
        return [
            jnp.sum(parts[i] + got[slot, i], axis=(0, 1), keepdims=True) for i in range(count)
        ]

    for g in range(chunks):
        own_copies[g].wait()
        sends[g].wait_recv()
        contract(g)
    finish_image()
    num = jnp.zeros((rows, blk), F32)
    den = jnp.zeros((rows, blk), F32)
    for g in range(chunks):
        own = x[g][0:2].astype(F32)
        num = num + fold(own * img[:, rows_of(g), :])
        den = den + fold(own * own)
    num, den = pair_total(0, [num, den])
    energy_one = num / den

    for copy in sends:
        copy.wait_send()
    den = jnp.zeros((rows, blk), F32)
    sends = [exchange(g, x[g].at[pl.ds(0, 2)]) for g in range(chunks)]
    for g in range(chunks):
        own = x[g][0:2].astype(F32)
        first = (own - STEP_SIZE * (img[:, rows_of(g), :] - energy_one * own)).astype(BF16)
        x[g][0:2] = first
        sends[g].start()
        first = first.astype(F32)
        den = den + fold(first * first)

    for g in range(chunks):
        sends[g].wait_recv()
        contract(g)
    finish_image()
    num = jnp.zeros((rows, blk), F32)
    for g in range(chunks):
        num = num + fold(x[g][0:2].astype(F32) * img[:, rows_of(g), :])
    num, den = pair_total(1, [num, den])
    energy_two = num / den

    norm = jnp.zeros((rows, blk), F32)
    for g in range(chunks):
        line = g * rows + lax.broadcasted_iota(jnp.int32, (rows, wide), 0)
        first = x[g][0:2].astype(F32)
        kept = first - STEP_SIZE * (img[:, rows_of(g), :] - energy_two * first)
        kept = jnp.stack(
            [jnp.where(line < ranks_ref[0, b], kept[b], 0.0) for b in range(2)], axis=0
        )
        img[:, rows_of(g), :] = kept
        norm = norm + fold(kept * kept)
    (norm,) = pair_total(2, [norm])
    cells = float(4 * blk * wide)
    scale = jnp.sqrt(cells / (norm + EPSILON))
    for b in range(2):

        def turn(p, carry):
            cols = pl.ds(pl.multiple_of(p * blk, blk), blk)
            tile = img[b, :, cols] * scale
            rounded = tile.astype(BF16)
            wave[0, b, :, cols] = rounded
            wave[1, b, :, cols] = tile.T.astype(BF16)
            return carry

        lax.fori_loop(0, phys, turn, 0, unroll=2)
    new_copy = pltpu.make_async_copy(wave.at[0], new_ref.at[0], in_sem.at[2])
    new_copy.start()

    env_scale = 1.0 / math.sqrt(wide)
    first_side = 1 - lax.rem(seg, 2)

    def boundary(side, pair):
        channels = pl.ds(2 * pair, 2)
        target = lax.rem(seg + 1 - 2 * side + segs, segs)
        return pltpu.make_async_remote_copy(
            src_ref=outbuf.at[side, channels],
            dst_ref=recv_ref.at[side, channels],
            send_sem=es_sem.at[side, pair],
            recv_sem=er_sem.at[side, pair],
            device_id=(target, group),
            device_id_type=MESH,
        )

    for turn_index in range(2):
        side = first_side if turn_index == 0 else 1 - first_side

        def one_pair(pair, carry):
            for b in range(2):
                ends = jnp.concatenate([env[side, 2 * pair, b], env[side, 2 * pair + 1, b]], axis=0)
                for n in range(phys // 2):
                    part = dot(ends, wave[side, b, :, 2 * n * blk : (2 * n + 2) * blk]).astype(BF16)
                    for i in range(2):
                        for j in range(2):
                            mixbuf[
                                b,
                                (2 * n + j) * blk : (2 * n + j + 1) * blk,
                                i * blk : (i + 1) * blk,
                            ] = part[i * blk : (i + 1) * blk, j * blk : (j + 1) * blk]
            for b in range(2):
                result = (dot(wave[1 - side, b], mixbuf[b]) * env_scale).astype(BF16)
                for i in range(2):
                    outbuf[side, 2 * pair + i, b] = result[:, i * blk : (i + 1) * blk]
            boundary(side, pair).start()
            return carry

        lax.fori_loop(0, pairs, one_pair, 0)

    for copy in sends:
        copy.wait_send()
    new_copy.wait()

    def settle(pair, carry):
        for side in range(2):
            boundary(side, pair).wait()
        return carry

    lax.fori_loop(0, pairs, settle, 0)


def solution(mesh):
    segs = mesh.shape["seg"]

    def shards(state, left_env, right_env, site_ops, sector_map, ranks):
        chan, _, blk, _ = left_env.shape[1:]
        phys = site_ops.shape[2]
        rows = 16
        chunks = blk // rows
        wide = phys * blk
        dims = (segs, chan, phys, blk, rows, chunks)
        anywhere = pl.BlockSpec(memory_space=pl.ANY)
        in_vmem = pl.BlockSpec(memory_space=pltpu.VMEM)
        in_smem = pl.BlockSpec(memory_space=pltpu.SMEM)
        dma = pltpu.SemaphoreType.DMA
        new_state, received = pl.pallas_call(
            functools.partial(kernel, dims),
            out_shape=(
                jax.ShapeDtypeStruct(state.shape, BF16),
                jax.ShapeDtypeStruct((2, chan, 2, blk, blk), BF16),
            ),
            in_specs=[anywhere, anywhere, anywhere, in_vmem, in_smem, in_smem],
            out_specs=(anywhere, anywhere),
            scratch_shapes=[pltpu.VMEM((4, rows, wide), BF16) for _ in range(chunks)]
            + [
                pltpu.VMEM((2, chan, 2, blk, blk), BF16),
                pltpu.VMEM((2, blk, chan * blk), BF16),
                pltpu.VMEM((chan, phys * rows, phys * rows), BF16),
                pltpu.VMEM((chan, 2 * blk, 2 * blk), BF16),
                pltpu.VMEM((2, chan * blk, wide), BF16),
                pltpu.VMEM((2, blk, wide), F32),
                pltpu.VMEM((2, 2, blk, wide), BF16),
                pltpu.VMEM((2, wide, 2 * blk), BF16),
                pltpu.VMEM((2, chan, 2, blk, blk), BF16),
                pltpu.VMEM((3, 2, rows, blk), F32),
                pltpu.VMEM((3, 2, rows, blk), F32),
                dma((3,)),
                dma((chunks,)),
                dma((chunks,)),
                dma((chunks,)),
                dma((2, chan // 2)),
                dma((2, chan // 2)),
                dma((3,)),
                dma((3,)),
            ],
            compiler_params=pltpu.CompilerParams(
                collective_id=0, has_side_effects=True, vmem_limit_bytes=60 * 1024 * 1024
            ),
        )(state, left_env, right_env, site_ops, sector_map, ranks)
        seg = lax.axis_index("seg")
        from_left = jnp.where(seg == 0, 0.0, received[0].astype(F32))
        from_right = jnp.where(seg == segs - 1, 0.0, received[1].astype(F32))
        return (new_state, from_left[None], from_right[None])

    placed = (
        P("seg", "blk", None, None),
        P("seg", None, "blk", None, None),
        P("seg", None, "blk", None, None),
        P("seg", None, None, None),
        P("seg", None, None),
        P("seg", "blk"),
    )
    return jax.shard_map(
        shards,
        mesh=mesh,
        in_specs=placed,
        out_specs=(
            P("seg", "blk", None, None),
            P("seg", None, "blk", None, None),
            P("seg", None, "blk", None, None),
        ),
        check_vma=False,
    )
```

profile of v0, /device:TPU:1, one launch (start us, length us, event | category | flops | bytes accessed | tf_op | source)
XLA Modules:
  0.0 112.3 jit_solution(10413052175265446536)
XLA Ops:
  0.6 1.4 %copy.9.refs_4_ = s32[1,14,4]{2,1,0:T(8,128)} copy(s32[1,14,4]{1,2,0:T(4,128)} %param.10) | data formatting | bytes 448 | tf_op args[4]
  2.0 105.4 %shard_map.85 = (bf16[1,2,128,2048]{3,2,1,0:T(8,128)(2,1)}, bf16[2,14,2,128,128]{4,3,2,1,0:T(8,128)(2,1)}) custom-call(bf16[1,2,128,2048]{3,2,1,0:T(8,128)(2,1)} %refs_0_.1, bf16[1,14,2,128,128]{4,3,2,1,0:T(8,128)(2,1)} %refs_1_.1, bf16[1,14,2,128,128]{4,3,2,1,0:T(8,128)(2,1)} %refs_2_.1, bf16[1,14,16,16]{3,2,1,0:T(8,128)(2,1)} %refs_3_.1, ...), custom_call_target="tpu_custom_call" | custom-call | tf_op jit(solution)/shard_map/pallas_call | solution.py:294
  107.5 0.0 copy-start
  107.5 3.9 %convert_select_fusion = (f32[1,14,2,128,128]{4,3,2,1,0:T(8,128)}, f32[1,14,2,128,128]{4,3,2,1,0:T(8,128)}) fusion(bf16[2,14,2,128,128]{4,3,2,1,0:T(8,128)(2,1)} %get-tuple-element.6, pred[]{:T(512)S(6)} %eq.7, pred[]{:T(512)S(6)} %eq.6), kind=kLoop, calls=%fused_computation | loop fusion | flops 1835008 | bytes 5505026 | tf_op jit(solution)/shard_map/jit(_where)/select_n | solution.py:330
  111.3 0.0 copy-done
  111.3 1.0 copy.11
Async XLA Ops:
  107.5 3.9 %copy-start = (bf16[1,2,128,2048]{3,2,1,0:T(8,128)(2,1)S(1)}, bf16[1,2,128,2048]{3,2,1,0:T(8,128)(2,1)}, u32[]{:S(2)}) copy-start(bf16[1,2,128,2048]{3,2,1,0:T(8,128)(2,1)} %get-tuple-element.12) | copy-start | bytes 3145732
where the time goes:
time: 113 us; the launch traced here: 112 us
  Pallas kernels  105 us (93%)
  other arithmetic  3.86 us (3%)
  local copies, waits for them, and re-layouts  2.34 us (2%)
    pallas_call x1, Pallas kernels, shards(): pl.pallas_call(functools.partial(kernel, dims), out_shape=(jax.ShapeDtype...  105 us
    select_n x1, other arithmetic, shards(): from_right = jnp.where(seg == segs - 1, 0.0, received[1].astype(F32))  3.86 us
    unnamed x4, local copies, waits for them, and re-layouts  2.34 us

commit v1 on v0

--- a/solution.py
+++ b/solution.py
@@ -24,10 +24,13 @@
     wide = phys * blk
     tall = phys * rows
     pairs = chan // 2
-    (state_ref, left_ref, right_ref, ops_ref, map_ref, ranks_ref, new_ref, recv_ref) = refs[:8]
+    (state_ref, left_ref, right_ref, ops_in, map_in, ranks_in, new_ref, recv_ref) = refs[:8]
     x = refs[8 : 8 + chunks]
-    (env, lcat, kron, rdiag, z, img, wave, mixbuf, outbuf, sums, got) = refs[8 + chunks : 19 + chunks]
-    (in_sem, own_sem, xs_sem, xr_sem, es_sem, er_sem, ss_sem, sr_sem) = refs[19 + chunks :]
+    y = refs[8 + chunks : 8 + 2 * chunks]
+    rest = refs[8 + 2 * chunks :]
+    (env, lcat, kron, rdiag, z, img, imgb, wave, mixbuf, outbuf, sums, got) = rest[:12]
+    (ops_ref, map_ref, ranks_ref) = rest[12:15]
+    (in_sem, own_sem, xs_sem, xr_sem, ys_sem, yr_sem, es_sem, er_sem, ss_sem, sr_sem) = rest[15:]
 
     seg = lax.axis_index("seg")
     group = lax.axis_index("blk")
@@ -47,15 +50,16 @@
     barrier = pltpu.get_barrier_semaphore()
     for where in ((seg, other), (following, group), (previous, group)):
         pl.semaphore_signal(barrier, inc=1, device_id=where, device_id_type=MESH)
-    right_copy.start()
-    left_copy.start()
-    for copy in own_copies:
+    ops_copy = pltpu.make_async_copy(ops_in.at[0], ops_ref, in_sem.at[3])
+    map_copy = pltpu.make_async_copy(map_in, map_ref, in_sem.at[4])
+    ranks_copy = pltpu.make_async_copy(ranks_in, ranks_ref, in_sem.at[5])
+    for copy in [ops_copy, right_copy, left_copy, map_copy, ranks_copy] + own_copies:
         copy.start()
     pl.semaphore_wait(barrier, 3)
 
-    def exchange(g, source):
+    def exchange(g):
         return pltpu.make_async_remote_copy(
-            src_ref=source,
+            src_ref=state_ref.at[0, :, pl.ds(g * rows, rows), :],
             dst_ref=x[g].at[pl.ds(2, 2)],
             send_sem=xs_sem.at[g],
             recv_sem=xr_sem.at[g],
@@ -63,7 +67,17 @@
             device_id_type=MESH,
         )
 
-    sends = [exchange(g, state_ref.at[0, :, pl.ds(g * rows, rows), :]) for g in range(chunks)]
+    def exchange_image(b, g):
+        return pltpu.make_async_remote_copy(
+            src_ref=imgb.at[b, pl.ds(g * rows, rows), :],
+            dst_ref=y[g].at[b],
+            send_sem=ys_sem.at[b, g],
+            recv_sem=yr_sem.at[b, g],
+            device_id=partner,
+            device_id_type=MESH,
+        )
+
+    sends = [exchange(g) for g in range(chunks)]
     for copy in sends:
         copy.start()
 
@@ -77,8 +91,10 @@
         lax.broadcasted_iota(jnp.int32, (tall, tall), 1) % rows
     )
 
+    ops_copy.wait()
+
     def build_kron(k, carry):
-        tall_op = dot(spread_rows, ops_ref[0, k]).astype(BF16)
+        tall_op = dot(spread_rows, ops_ref[k]).astype(BF16)
         full = dot(tall_op, spread_cols)
         kron[k] = jnp.where(same, full, 0.0).astype(BF16)
         return carry
@@ -97,6 +113,8 @@
 
     lax.fori_loop(0, chan, build_rdiag, 0)
 
+    map_copy.wait()
+    ranks_copy.wait()
     left_copy.wait()
     for k in range(chan):
         for b in range(2):
@@ -108,7 +126,7 @@
     def contract(g):
         def one(k, carry):
             spots = [
-                lax.rem(map_ref[0, k, 2 * group + b] + 4 - 2 * group, 4) for b in range(2)
+                lax.rem(map_ref[0, 2 * group + b, k] + 4 - 2 * group, 4) for b in range(2)
             ]
             source = jnp.concatenate(
                 [jnp.concatenate(tiles(x[g][spot]), axis=0) for spot in spots], axis=1
@@ -125,15 +143,20 @@
 
         lax.fori_loop(0, chan, one, 0, unroll=2)
 
-    def finish_image():
-        for b in range(2):
-
-            def one(n, carry):
-                cols = pl.ds(pl.multiple_of(n * 256, 256), 256)
-                img[b, :, cols] = dot(lcat[b], z[b, :, cols])
-                return carry
-
-            lax.fori_loop(0, wide // 256, one, 0)
+    def finish_image(b, num, keep_rounded):
+        def one(n, carry):
+            start = pl.multiple_of(n * 256, 256)
+            cols = pl.ds(start, 256)
+            tile = dot(lcat[b], z[b, :, cols])
+            img[b, :, cols] = tile
+            if keep_rounded:
+                imgb[b, :, cols] = tile.astype(BF16)
+            for g in range(chunks):
+                part = x[g][b, :, cols].astype(F32) * tile[g * rows : (g + 1) * rows, :]
+                carry = carry + part[:, :blk] + part[:, blk:]
+            return carry
+
+        return lax.fori_loop(0, wide // 256, one, num)
 
     def fold(product):
         both = product[0] + product[1]
@@ -145,80 +168,105 @@
     def rows_of(g):
         return slice(g * rows, (g + 1) * rows)
 
-    def pair_total(slot, parts):
+    def send_sums(slot, parts):
         for i, part in enumerate(parts):
             sums[slot, i] = part
-        count = len(parts)
         copy = pltpu.make_async_remote_copy(
-            src_ref=sums.at[slot, pl.ds(0, count)],
-            dst_ref=got.at[slot, pl.ds(0, count)],
+            src_ref=sums.at[slot, pl.ds(0, len(parts))],
+            dst_ref=got.at[slot, pl.ds(0, len(parts))],
             send_sem=ss_sem.at[slot],
             recv_sem=sr_sem.at[slot],
             device_id=partner,
             device_id_type=MESH,
         )
         copy.start()
-        copy.wait()
-        return [
-            jnp.sum(parts[i] + got[slot, i], axis=(0, 1), keepdims=True) for i in range(count)
-        ]
-
+        return copy
+
+    def total_of(part):
+        return jnp.sum(part, axis=(0, 1), keepdims=True)
+
+    den = jnp.zeros((rows, blk), F32)
     for g in range(chunks):
         own_copies[g].wait()
+        own = x[g][0:2].astype(F32)
+        den = den + fold(own * own)
         sends[g].wait_recv()
         contract(g)
-    finish_image()
-    num = jnp.zeros((rows, blk), F32)
+    num = finish_image(0, jnp.zeros((rows, blk), F32), True)
+    images = [[exchange_image(b, g) for g in range(chunks)] for b in range(2)]
+    for g in range(2):
+        images[0][g].start()
+    num = finish_image(1, num, True)
+    message = send_sums(0, [num, den])
+    for g in range(2):
+        images[1][g].start()
+    for g in range(2, chunks):
+        for b in range(2):
+            images[b][g].start()
+    message.wait()
+    energy_one = total_of(num + got[0, 0]) / total_of(den + got[0, 1])
+
     den = jnp.zeros((rows, blk), F32)
-    for g in range(chunks):
-        own = x[g][0:2].astype(F32)
-        num = num + fold(own * img[:, rows_of(g), :])
-        den = den + fold(own * own)
-    num, den = pair_total(0, [num, den])
-    energy_one = num / den
-
-    for copy in sends:
-        copy.wait_send()
-    den = jnp.zeros((rows, blk), F32)
-    sends = [exchange(g, x[g].at[pl.ds(0, 2)]) for g in range(chunks)]
     for g in range(chunks):
         own = x[g][0:2].astype(F32)
         first = (own - STEP_SIZE * (img[:, rows_of(g), :] - energy_one * own)).astype(BF16)
         x[g][0:2] = first
-        sends[g].start()
         first = first.astype(F32)
         den = den + fold(first * first)
 
     for g in range(chunks):
-        sends[g].wait_recv()
+        for b in range(2):
+            images[b][g].wait_recv()
+        theirs = x[g][2:4].astype(F32)
+        x[g][2:4] = (theirs - STEP_SIZE * (y[g][...].astype(F32) - energy_one * theirs)).astype(BF16)
         contract(g)
-    finish_image()
     num = jnp.zeros((rows, blk), F32)
-    for g in range(chunks):
-        num = num + fold(x[g][0:2].astype(F32) * img[:, rows_of(g), :])
-    num, den = pair_total(1, [num, den])
-    energy_two = num / den
-
-    norm = jnp.zeros((rows, blk), F32)
+    for b in range(2):
+        num = finish_image(b, num, False)
+
+    def quotient(top, bottom):
+        top, bottom = total_of(top), total_of(bottom)
+        return jnp.where(bottom > 0.0, top / bottom, 0.0)
+
+    near = quotient(num, den)
+    square = jnp.zeros((rows, blk), F32)
+    cross = jnp.zeros((rows, blk), F32)
+    start = jnp.zeros((rows, blk), F32)
     for g in range(chunks):
         line = g * rows + lax.broadcasted_iota(jnp.int32, (rows, wide), 0)
         first = x[g][0:2].astype(F32)
-        kept = first - STEP_SIZE * (img[:, rows_of(g), :] - energy_two * first)
-        kept = jnp.stack(
-            [jnp.where(line < ranks_ref[0, b], kept[b], 0.0) for b in range(2)], axis=0
-        )
+        first = jnp.stack(
+            [jnp.where(line < ranks_ref[0, b], first[b], 0.0) for b in range(2)], axis=0
+        )
+        image = jnp.stack(
+            [jnp.where(line < ranks_ref[0, b], img[b, rows_of(g), :], 0.0) for b in range(2)], axis=0
+        )
+        kept = first - STEP_SIZE * (image - near * first)
         img[:, rows_of(g), :] = kept
-        norm = norm + fold(kept * kept)
-    (norm,) = pair_total(2, [norm])
+        square = square + fold(kept * kept)
+        cross = cross + fold(kept * first)
+        start = start + fold(first * first)
+    send_sums(1, [num, den, square, cross, start]).wait()
+    energy_two = total_of(num + got[1, 0]) / total_of(den + got[1, 1])
+
+    def square_at(step, a, b, c):
+        return total_of(a) + step * (0.5 * total_of(b) + 0.0625 * (step * total_of(c)))
+
+    shift = energy_two - near
+    far = energy_two - quotient(got[1, 0], got[1, 1])
+    norm = square_at(shift, square, cross, start) + square_at(far, got[1, 2], got[1, 3], got[1, 4])
+    norm = jnp.maximum(norm, 0.0)
     cells = float(4 * blk * wide)
     scale = jnp.sqrt(cells / (norm + EPSILON))
     for b in range(2):
+        inside = lax.broadcasted_iota(jnp.int32, (blk, blk), 0) < ranks_ref[0, b]
 
         def turn(p, carry):
             cols = pl.ds(pl.multiple_of(p * blk, blk), blk)
-            tile = img[b, :, cols] * scale
-            rounded = tile.astype(BF16)
-            wave[0, b, :, cols] = rounded
+            first = jnp.concatenate([x[g][b, :, cols] for g in range(chunks)], axis=0)
+            first = jnp.where(inside, first.astype(F32), 0.0)
+            tile = (img[b, :, cols] + (STEP_SIZE * shift) * first) * scale
+            wave[0, b, :, cols] = tile.astype(BF16)
             wave[1, b, :, cols] = tile.T.astype(BF16)
             return carry
 
@@ -265,7 +313,7 @@
 
         lax.fori_loop(0, pairs, one_pair, 0)
 
-    for copy in sends:
+    for copy in sends + images[0] + images[1]:
         copy.wait_send()
     new_copy.wait()
 
@@ -288,8 +336,6 @@
         wide = phys * blk
         dims = (segs, chan, phys, blk, rows, chunks)
         anywhere = pl.BlockSpec(memory_space=pl.ANY)
-        in_vmem = pl.BlockSpec(memory_space=pltpu.VMEM)
-        in_smem = pl.BlockSpec(memory_space=pltpu.SMEM)
         dma = pltpu.SemaphoreType.DMA
         new_state, received = pl.pallas_call(
             functools.partial(kernel, dims),
@@ -297,9 +343,10 @@
                 jax.ShapeDtypeStruct(state.shape, BF16),
                 jax.ShapeDtypeStruct((2, chan, 2, blk, blk), BF16),
             ),
-            in_specs=[anywhere, anywhere, anywhere, in_vmem, in_smem, in_smem],
+            in_specs=[anywhere] * 6,
             out_specs=(anywhere, anywhere),
             scratch_shapes=[pltpu.VMEM((4, rows, wide), BF16) for _ in range(chunks)]
+            + [pltpu.VMEM((2, rows, wide), BF16) for _ in range(chunks)]
             + [
                 pltpu.VMEM((2, chan, 2, blk, blk), BF16),
                 pltpu.VMEM((2, blk, chan * blk), BF16),
@@ -307,24 +354,30 @@
                 pltpu.VMEM((chan, 2 * blk, 2 * blk), BF16),
                 pltpu.VMEM((2, chan * blk, wide), BF16),
                 pltpu.VMEM((2, blk, wide), F32),
+                pltpu.VMEM((2, blk, wide), BF16),
                 pltpu.VMEM((2, 2, blk, wide), BF16),
                 pltpu.VMEM((2, wide, 2 * blk), BF16),
                 pltpu.VMEM((2, chan, 2, blk, blk), BF16),
-                pltpu.VMEM((3, 2, rows, blk), F32),
-                pltpu.VMEM((3, 2, rows, blk), F32),
-                dma((3,)),
+                pltpu.VMEM((2, 5, rows, blk), F32),
+                pltpu.VMEM((2, 5, rows, blk), F32),
+                pltpu.VMEM((chan, phys, phys), BF16),
+                pltpu.SMEM((1, 4, chan), jnp.int32),
+                pltpu.SMEM((1, 2), jnp.int32),
+                dma((6,)),
                 dma((chunks,)),
                 dma((chunks,)),
                 dma((chunks,)),
+                dma((2, chunks)),
+                dma((2, chunks)),
                 dma((2, chan // 2)),
                 dma((2, chan // 2)),
-                dma((3,)),
-                dma((3,)),
+                dma((2,)),
+                dma((2,)),
             ],
             compiler_params=pltpu.CompilerParams(
                 collective_id=0, has_side_effects=True, vmem_limit_bytes=60 * 1024 * 1024
             ),
-        )(state, left_env, right_env, site_ops, sector_map, ranks)
+        )(state, left_env, right_env, site_ops, jnp.swapaxes(sector_map, 1, 2), ranks)
         seg = lax.axis_index("seg")
         from_left = jnp.where(seg == 0, 0.0, received[0].astype(F32))
         from_right = jnp.where(seg == segs - 1, 0.0, received[1].astype(F32))

time: 113 us -> 107 us (0.947)
  Pallas kernels: 105 us -> 102 us
  local copies, waits for them, and re-layouts: 2.34 us -> 0.97 us
    pallas_call x1, Pallas kernels: 105 us -> 102 us  [shards(): pl.pallas_call(functools.partial(kernel, dims), out_shape=(jax.ShapeDtype...]
    unnamed x4 -> x3, local copies, waits for them, and re-layouts: 2.34 us -> 0.97 us
where the time goes in v1:
time: 107 us
  Pallas kernels  102 us (95%)
  other arithmetic  3.86 us (4%)
    pallas_call x1, Pallas kernels, shards(): pl.pallas_call(functools.partial(kernel, dims), out_shape=(jax.ShapeDtype...  102 us
    select_n x1, other arithmetic, shards(): from_right = jnp.where(seg == segs - 1, 0.0, received[1].astype(F32))  3.86 us

profile of v1, /device:TPU:1, one launch (start us, length us, event | category | flops | bytes accessed | tf_op | source)
XLA Modules:
  0.0 107.3 jit_solution(15608070754895808203)
XLA Ops:
  0.6 101.8 %shard_map.85 = (bf16[1,2,128,2048]{3,2,1,0:T(8,128)(2,1)}, bf16[2,14,2,128,128]{4,3,2,1,0:T(8,128)(2,1)}) custom-call(bf16[1,2,128,2048]{3,2,1,0:T(8,128)(2,1)} %refs_0_.1, bf16[1,14,2,128,128]{4,3,2,1,0:T(8,128)(2,1)} %refs_1_.1, bf16[1,14,2,128,128]{4,3,2,1,0:T(8,128)(2,1)} %refs_2_.1, bf16[1,14,16,16]{3,2,1,0:T(8,128)(2,1)} %refs_3_.1, ...), custom_call_target="tpu_custom_call" | custom-call | tf_op jit(solution)/shard_map/pallas_call | solution.py:340
  102.4 0.0 copy-start
  102.4 3.9 %convert_select_fusion = (f32[1,14,2,128,128]{4,3,2,1,0:T(8,128)}, f32[1,14,2,128,128]{4,3,2,1,0:T(8,128)}) fusion(bf16[2,14,2,128,128]{4,3,2,1,0:T(8,128)(2,1)} %get-tuple-element.6, pred[]{:T(512)S(6)} %eq.7, pred[]{:T(512)S(6)} %eq.6), kind=kLoop, calls=%fused_computation | loop fusion | flops 1835008 | bytes 5505026 | tf_op jit(solution)/shard_map/jit(_where)/select_n | solution.py:383
  106.3 0.0 copy-done
  106.3 1.0 copy.10
Async XLA Ops:
  102.4 3.9 %copy-start = (bf16[1,2,128,2048]{3,2,1,0:T(8,128)(2,1)S(1)}, bf16[1,2,128,2048]{3,2,1,0:T(8,128)(2,1)}, u32[]{:S(2)}) copy-start(bf16[1,2,128,2048]{3,2,1,0:T(8,128)(2,1)} %get-tuple-element.12) | copy-start | bytes 3145732

commit v2 on v1

--- a/solution.py
+++ b/solution.py
@@ -141,7 +141,7 @@
                     ]
             return carry
 
-        lax.fori_loop(0, chan, one, 0, unroll=2)
+        lax.fori_loop(0, chan, one, 0, unroll=7)
 
     def finish_image(b, num, keep_rounded):
         def one(n, carry):

time: 107 us -> 99.7 us (0.932)
  Pallas kernels: 102 us -> 94.1 us
    pallas_call x1, Pallas kernels: 102 us -> 94.1 us  [shards(): pl.pallas_call(functools.partial(kernel, dims), out_shape=(jax.ShapeDtype...]
where the time goes in v2:
time: 99.7 us; the launch traced here: 99.6 us
  Pallas kernels  94.1 us (94%)
  other arithmetic  3.86 us (4%)
    pallas_call x1, Pallas kernels, shards(): pl.pallas_call(functools.partial(kernel, dims), out_shape=(jax.ShapeDtype...  94.1 us
    select_n x1, other arithmetic, shards(): from_right = jnp.where(seg == segs - 1, 0.0, received[1].astype(F32))  3.86 us

profile of v2, /device:TPU:1, one launch (start us, length us, event | category | flops | bytes accessed | tf_op | source)
XLA Modules:
  0.0 99.6 jit_solution(705011814532000328)
XLA Ops:
  0.6 94.1 %shard_map.85 = (bf16[1,2,128,2048]{3,2,1,0:T(8,128)(2,1)}, bf16[2,14,2,128,128]{4,3,2,1,0:T(8,128)(2,1)}) custom-call(bf16[1,2,128,2048]{3,2,1,0:T(8,128)(2,1)} %refs_0_.1, bf16[1,14,2,128,128]{4,3,2,1,0:T(8,128)(2,1)} %refs_1_.1, bf16[1,14,2,128,128]{4,3,2,1,0:T(8,128)(2,1)} %refs_2_.1, bf16[1,14,16,16]{3,2,1,0:T(8,128)(2,1)} %refs_3_.1, ...), custom_call_target="tpu_custom_call" | custom-call | tf_op jit(solution)/shard_map/pallas_call | solution.py:340
  94.7 0.0 copy-start
  94.7 3.9 %convert_select_fusion = (f32[1,14,2,128,128]{4,3,2,1,0:T(8,128)}, f32[1,14,2,128,128]{4,3,2,1,0:T(8,128)}) fusion(bf16[2,14,2,128,128]{4,3,2,1,0:T(8,128)(2,1)} %get-tuple-element.6, pred[]{:T(512)S(6)} %eq.7, pred[]{:T(512)S(6)} %eq.6), kind=kLoop, calls=%fused_computation | loop fusion | flops 1835008 | bytes 5505026 | tf_op jit(solution)/shard_map/jit(_where)/select_n | solution.py:383
  98.6 0.0 copy-done
  98.6 1.0 copy.10
Async XLA Ops:
  94.7 3.9 %copy-start = (bf16[1,2,128,2048]{3,2,1,0:T(8,128)(2,1)S(1)}, bf16[1,2,128,2048]{3,2,1,0:T(8,128)(2,1)}, u32[]{:S(2)}) copy-start(bf16[1,2,128,2048]{3,2,1,0:T(8,128)(2,1)} %get-tuple-element.12) | copy-start | bytes 3145732
